TPU v7x, 32 devices: a whole 2x2x4 slice. The times are simulated.
32 devices in a mesh: bulk: 8 (over z, x), contact: 4 (over y, core).
Axes of the slice: x: 2, y: 2, z: 4, core: 2. Of those that a mesh axis runs over, the one named last changes fastest.
Arguments:
- k_inv: float32 [65536, 2048], P(('bulk', 'contact'))
- mortar_slave: float32 [8192, 256], P(('bulk', 'contact')), may hold values from -0.375 to 0.375
- mortar_master: float32 [8192, 256], P(('bulk', 'contact')), may hold values from -0.375 to 0.375
- force: float32 [65536, 256], P(('bulk', 'contact')), may hold values from -6 to 6
- lam_glue: float32 [8192, 256], P(('bulk', 'contact')), may hold values from -6 to 6
- lam_contact: float32 [8192, 256], P(('bulk', 'contact')), may hold values from 0 to 1
- master_map: int32 [32], P(('bulk', 'contact')), may hold values from 0 to 3, as said below
- on_surface: int32 [32], P(('bulk', 'contact')), may hold values 0 or 1
- step_type: int32 [2, 256], replicated, may hold values from 0 to 2
- active: int32 [2, 8192, 256], P(None, ('bulk', 'contact')), may hold values 0 or 1
- expand_len: float32 [256], replicated, may hold values from 0.05 to 0.3
Outputs:
- glue_final: float32 [8192, 256], P(('bulk', 'contact'))
- contact_final: float32 [8192, 256], P(('bulk', 'contact'))
- grad_glue_final: float32 [8192, 256], P(('bulk', 'contact'))
- grad_contact_final: float32 [8192, 256], P(('bulk', 'contact'))
Inputs may be any that keep to these rules, and one draw needn't show every extreme that they name: master_map never names the subdomain's own position in its group of 4.
All inputs are finite; a program needn't handle non-finite values. No bound on the sum of `on_surface` or of `active` on one device may be relied on, other than what follows from the above.
Results may differ from a plain program's by a relative error of at most 0.0003.
Values sent between devices are 32-bit elements; how exact they have to be, the bound alone decides.
A program may use at most 128 MiB of HBM per device.

v0:
```python
import functools

import jax
import jax.numpy as jnp
from jax import lax
from jax.experimental import pallas as pl
from jax.experimental.pallas import tpu as pltpu
from jax.sharding import PartitionSpec as P

MESH = pl.DeviceIdType.MESH
F32 = jnp.float32
BF16 = jnp.bfloat16


def split(x):
    high = x.astype(BF16)
    return high, (x - high.astype(F32)).astype(BF16)


def bdot(a, b):
    return jnp.dot(a, b, preferred_element_type=F32)


def dot3(a_high, a_low, x):
    width = x.shape[1]
    high, low = split(x)
    both = bdot(a_high, jnp.concatenate([high, low], axis=1))
    return both[:, :width] + (both[:, width:] + bdot(a_low, high))


def kernel(
    n_bulk, n_group,
    master_ref, surface_ref, kinv_ref, ms_ref, mm_ref, force_ref, lamg_ref, lamc_ref, kinds_ref, active_ref, expand_ref,
    outg_ref, outc_ref, outgg_ref, outgc_ref,
    k_raw, k_hi, k_lo, f_raw, f_hi, f_lo, base, gap_hi, gap_lo, adj_hi, adj_lo,
    w_ref, wfix, y_ref, gp, gl, zg, zc, tsrc, tslots, cslots, dg, dc, gg, gc, imz_g, imz_c, meta_src, meta,
    r1, r2,
    load_sem, gp_send, gp_recv, gl_send, gl_recv, t_send, t_recv, c_send, c_recv, m_send, m_recv,
    r1_send, r1_recv, r2_send, r2_recv,
):
    face, columns = lamg_ref.shape
    mortar = lamc_ref.shape[0]
    rows = 2 * face + mortar
    half = columns // 2
    b = lax.axis_index("bulk")
    c = lax.axis_index("contact")
    pairs = n_group // 2
    q = lax.div(c, 2)
    r = lax.rem(c, 2)
    partner = 2 * q + 1 - r
    pending = []

    barrier = pltpu.get_barrier_semaphore()
    for k in range(1, n_group):
        pl.semaphore_signal(barrier, inc=1, device_id={"bulk": b, "contact": lax.rem(c + k, n_group)}, device_id_type=MESH)
    for k in range(1, n_bulk):
        pl.semaphore_signal(barrier, inc=1, device_id={"bulk": lax.rem(b + k, n_bulk), "contact": c}, device_id_type=MESH)
    load_k = pltpu.make_async_copy(kinv_ref.at[pl.ds(0, rows)], k_raw, load_sem.at[0])
    load_f = pltpu.make_async_copy(force_ref, f_raw, load_sem.at[1])
    load_k.start()
    load_f.start()

    slot_ids = [partner]
    for k in range(1, pairs):
        there = lax.rem(q - k + pairs, pairs)
        slot_ids += [2 * there + r, 2 * there + 1 - r]

    def remote(src, dst, send, recv, where):
        return pltpu.make_async_remote_copy(
            src_ref=src, dst_ref=dst, send_sem=send, recv_sem=recv, device_id=where, device_id_type=MESH
        )

    def begin(copy):
        copy.start()
        pending.append(copy)

    def gather_start(src, slots, send, recv):
        for k in range(1, pairs):
            begin(remote(src, slots.at[2 * k - 1], send.at[2 * k - 1], recv.at[2 * k - 1],
                         {"bulk": b, "contact": 2 * lax.rem(q + k, pairs) + r}))
        begin(remote(src, slots.at[0], send.at[0], recv.at[0], {"bulk": b, "contact": partner}))

    def gather_relay(slots, send, recv):
        for k in range(1, pairs):
            remote(slots.at[2 * k - 1], slots.at[2 * k - 1], send.at[2 * k - 1], recv.at[2 * k - 1],
                   {"bulk": b, "contact": partner}).wait_recv()
            begin(remote(slots.at[2 * k - 1], slots.at[2 * k], send.at[2 * k], recv.at[2 * k],
                         {"bulk": b, "contact": partner}))

    def gather_end(slots, send, recv):
        for i in [0] + [2 * k for k in range(1, pairs)]:
            remote(slots.at[i], slots.at[i], send.at[i], recv.at[i], {"bulk": b, "contact": partner}).wait_recv()

    right = {"bulk": lax.rem(b + 1, n_bulk), "contact": c}
    left = {"bulk": lax.rem(b + n_bulk - 1, n_bulk), "contact": c}
    has_right = b < n_bulk - 1
    has_left = b > 0
    late = []

    def push_glue(src, p, h):
        copy = remote(src, gp.at[p, h], gp_send.at[p, h], gp_recv.at[p, h], right)

        @pl.when(has_right)
        def _():
            copy.start()

        late.append((has_right, copy))

    def push_glue_end(p, h):
        @pl.when(has_left)
        def _():
            remote(gp.at[p, h], gp.at[p, h], gp_send.at[p, h], gp_recv.at[p, h], left).wait_recv()

    def pull_glue(src, p, h):
        copy = remote(src, gl.at[p, h], gl_send.at[p, h], gl_recv.at[p, h], left)

        @pl.when(has_left)
        def _():
            copy.start()

        late.append((has_left, copy))

    def pull_glue_end(p, h):
        @pl.when(has_right)
        def _():
            remote(gl.at[p, h], gl.at[p, h], gl_send.at[p, h], gl_recv.at[p, h], right).wait_recv()

    @pl.when(b == 0)
    def _():
        gp[...] = jnp.zeros_like(gp)

    @pl.when(b == n_bulk - 1)
    def _():
        gl[...] = jnp.zeros_like(gl)

    surface = surface_ref[0].astype(F32)
    own_master = jnp.full((8, half), master_ref[0].astype(F32), F32)
    meta_src[...] = own_master
    mask = jnp.where(has_right, 1.0, 0.0).astype(F32)
    slave = ms_ref[...] * surface
    master = mm_ref[...] * surface
    for i, part in enumerate((slave, -master)):
        high, low = split(part)
        gap_hi[:, i * mortar : (i + 1) * mortar] = high
        gap_lo[:, i * mortar : (i + 1) * mortar] = low
    for i, part in enumerate((slave, master)):
        high, low = split(part.T)
        adj_hi[i * mortar : (i + 1) * mortar, :] = high
        adj_lo[i * mortar : (i + 1) * mortar, :] = low

    def cols(h):
        return slice(h * half, (h + 1) * half)

    def send_mortar(dual, p, h):
        both = dot3(adj_hi[...], adj_lo[...], dual)
        tsrc[p, h] = both[mortar:]
        return both[:mortar]

    def mortar_start(p, h):
        gather_start(tsrc.at[p, h], tslots.at[p, h], t_send.at[p, h], t_recv.at[p, h])

    def mortar_end(p, h):
        gather_end(tslots.at[p, h], t_send.at[p, h], t_recv.at[p, h])
        total = 0.0
        for i in range(n_group - 1):
            total = total + jnp.where(meta[i, 0:1, :] == c.astype(F32), tslots[p, h, i], 0.0)
        return total

    def mortar_relay(p, h):
        gather_relay(tslots.at[p, h], t_send.at[p, h], t_recv.at[p, h])

    def face_start(p, h):
        gather_start(y_ref.at[p, h, pl.ds(2 * face, mortar)], cslots.at[p, h], c_send.at[p, h], c_recv.at[p, h])
        pull_glue(y_ref.at[p, h, pl.ds(0, face)], p, h)

    def face_relay(p, h):
        gather_relay(cslots.at[p, h], c_send.at[p, h], c_recv.at[p, h])

    def face_end(p, h):
        gather_end(cslots.at[p, h], c_send.at[p, h], c_recv.at[p, h])
        chosen = 0.0
        for i, ident in enumerate(slot_ids):
            chosen = chosen + jnp.where(own_master[0:1, :] == ident.astype(F32), cslots[p, h, i], 0.0)
        stacked = jnp.concatenate([y_ref[p, h, 2 * face :, :], chosen], axis=0)
        gap = dot3(gap_hi[...], gap_lo[...], stacked)
        pull_glue_end(p, h)
        return (y_ref[p, h, face : 2 * face, :] - gl[p, h]) * mask, gap

    def apply(w_value, p, h, first, plus):
        high, low = split(w_value)
        both = jnp.concatenate([high, low], axis=1)
        cut = pl.ds(first, w_value.shape[0])
        for i in range(3):
            at = pl.ds(i * face, face)
            out = bdot(k_hi[at, cut], both)
            out = out[:, :half] + (out[:, half:] + bdot(k_lo[at, cut], high))
            if plus:
                out = out + base[h, at, :]
            y_ref[p, h, at, :] = out

    def sums_start(n, h, values):
        padded = values + [jnp.zeros_like(values[0])] * (8 - len(values))
        r1[n, h, c] = jnp.concatenate(padded, axis=0)
        for k in range(1, n_group):
            begin(remote(r1.at[n, h, c], r1.at[n, h, c], r1_send.at[n, h, k], r1_recv.at[n, h, k],
                         {"bulk": b, "contact": lax.rem(c + k, n_group)}))

    def sums_mid(n, h):
        for k in range(1, n_group):
            there = lax.rem(c - k + n_group, n_group)
            remote(r1.at[n, h, there], r1.at[n, h, there], r1_send.at[n, h, k], r1_recv.at[n, h, k],
                   {"bulk": b, "contact": there}).wait_recv()
        r2[n, h, b] = jnp.sum(r1[n, h], axis=0)
        for k in range(1, n_bulk):
            begin(remote(r2.at[n, h, b], r2.at[n, h, b], r2_send.at[n, h, k], r2_recv.at[n, h, k],
                         {"bulk": lax.rem(b + k, n_bulk), "contact": c}))

    def sums_end(n, h):
        for k in range(1, n_bulk):
            there = lax.rem(b - k + n_bulk, n_bulk)
            remote(r2.at[n, h, there], r2.at[n, h, there], r2_send.at[n, h, k], r2_recv.at[n, h, k],
                   {"bulk": there, "contact": c}).wait_recv()
        return jnp.sum(r2[n, h], axis=0)

    def inner(*terms):
        return sum(jnp.sum(x * y, axis=0, keepdims=True) for x, y in terms)

    for h in range(2):
        w_ref[0, h, 2 * face :, :] = send_mortar(lamc_ref[:, cols(h)], 0, h)
    pl.semaphore_wait(barrier, n_group - 1 + n_bulk - 1)
    for i in range(n_group - 1):
        to = slot_ids[i]
        k = (i + 1) // 2
        mirror = i if i == 0 else 2 * (pairs - k) - (i % 2)
        begin(remote(meta_src, meta.at[mirror], m_send.at[i], m_recv.at[mirror], {"bulk": b, "contact": to}))
    for h in range(2):
        mortar_start(0, h)
        push_glue(lamg_ref.at[:, pl.ds(h * half, half)], 0, h)

    load_f.wait()
    high, low = split(-f_raw[...])
    f_hi[...] = high
    f_lo[...] = low
    load_k.wait()

    @pl.loop(0, 3)
    def _(i):
        at = pl.ds(pl.multiple_of(i * face, face), face)
        high, low = split(k_raw[at, :])
        k_hi[at, :] = high
        k_lo[at, :] = low
        out = bdot(k_hi[at, :], f_hi[...])
        out = out + (bdot(k_hi[at, :], f_lo[...]) + bdot(k_lo[at, :], f_hi[...]))
        for h in range(2):
            base[h, at, :] = out[:, h * half : (h + 1) * half]

    for i in range(n_group - 1):
        remote(meta.at[i], meta.at[i], m_send.at[i], m_recv.at[i], {"bulk": b, "contact": partner}).wait_recv()

    for h in range(2):
        mortar_relay(0, h)
        push_glue_end(0, h)
        own = w_ref[0, h, 2 * face :, :]
        w = jnp.concatenate([-gp[0, h], lamg_ref[:, cols(h)] * mask, own - mortar_end(0, h)], axis=0)
        apply(w, 0, h, 0, True)
        face_start(0, h)

    for h in range(2):
        face_relay(0, h)
        grad_g, grad_c = face_end(0, h)
        gg[h] = grad_g
        gc[h] = grad_c
        kind = kinds_ref[0:1, cols(h)]
        length = expand_ref[0:1, cols(h)]
        expand = kind == 1
        chop = kind == 2
        held = active_ref[0, :, cols(h)].astype(F32)
        dir_g = jnp.where(chop, 0.0, grad_g)
        dir_c = jnp.where(chop, jnp.minimum(grad_c, 0.0) * held, grad_c * (1.0 - held)) * surface
        scale = jnp.where(expand, length, 1.0)
        dg[h] = dir_g
        dc[h] = dir_c
        z_c = scale * dir_c
        fix = jnp.where(expand, surface * jnp.maximum(z_c - lamc_ref[:, cols(h)], 0.0), 0.0)
        zg[0, h] = scale * dir_g
        push_glue(zg.at[0, h], 1, h)
        zc[0, h] = z_c - fix
        w_ref[0, h, 2 * face :, :] = send_mortar(zc[0, h], 1, h)
        mortar_start(1, h)
        wfix[h] = send_mortar(fix, 2, h)
    for h in range(2):
        mortar_start(2, h)

    for h in range(2):
        mortar_relay(1, h)
        push_glue_end(1, h)
        own = w_ref[0, h, 2 * face :, :]
        w = jnp.concatenate([-gp[1, h], zg[0, h], own - mortar_end(1, h)], axis=0)
        w_ref[0, h] = w
        apply(w, 1, h, 0, False)
        face_start(1, h)
        sums_start(0, h, [
            inner((gg[h], dg[h]), (gc[h], dc[h])),
            inner((w, y_ref[1, h])),
        ])
    for h in range(2):
        mortar_relay(2, h)
        sums_mid(0, h)
    for h in range(2):
        w = wfix[h] - mortar_end(2, h)
        wfix[h] = w
        apply(w, 2, h, 2 * face, False)

    for h in range(2):
        face_relay(1, h)
        b_g, b_c = face_end(1, h)
        imz_g[h] = b_g
        imz_c[h] = b_c
        sums = sums_end(0, h)
        step = jnp.where(kinds_ref[0:1, cols(h)] == 1, 1.0, sums[0:1] / sums[1:2])
        grad_g = gg[h] - step * b_g
        grad_c = gc[h] - step * b_c
        lam_c = lamc_ref[:, cols(h)] - step * zc[0, h]
        outg_ref[:, cols(h)] = lamg_ref[:, cols(h)] * mask - step * zg[0, h]
        outc_ref[:, cols(h)] = lam_c
        gg[h] = grad_g
        gc[h] = grad_c
        kind = kinds_ref[1:2, cols(h)]
        expand = kind == 1
        chop = kind == 2
        held = active_ref[1, :, cols(h)].astype(F32)
        scale = jnp.where(expand, expand_ref[0:1, cols(h)], 1.0)
        zg[1, h] = jnp.where(chop, 0.0, scale * grad_g)
        push_glue(zg.at[1, h], 2, h)
        v_c = jnp.where(chop, jnp.minimum(grad_c, 0.0) * held, scale * (grad_c * (1.0 - held))) * surface
        zc[1, h] = v_c - jnp.where(expand, surface * jnp.maximum(v_c - lam_c, 0.0), 0.0)
        w_ref[1, h, 2 * face :, :] = send_mortar(zc[1, h], 3, h)
        mortar_start(3, h)
    for h in range(2):
        face_start(2, h)

    def scale_of(h):
        return jnp.where(kinds_ref[0:1, cols(h)] == 1, expand_ref[0:1, cols(h)], 1.0)

    for h in range(2):
        mortar_relay(3, h)
        push_glue_end(2, h)
        own = w_ref[1, h, 2 * face :, :]
        w = jnp.concatenate([-gp[2, h], zg[1, h], own - mortar_end(3, h)], axis=0)
        apply(w, 3, h, 0, False)
        face_start(3, h)
        w_0 = jnp.concatenate([w_ref[0, h, : 2 * face, :], w_ref[0, h, 2 * face :, :] + wfix[h]], axis=0)
        y_0 = y_ref[1, h] + y_ref[2, h]
        inverse = 1.0 / scale_of(h)
        y_v = y_ref[3, h]
        sums_start(1, h, [
            inner((w, y_0)) * inverse,
            inner((w, y_v)),
            inner((w_0, y_v)) * inverse,
            inner((gg[h], zg[1, h]), (gc[h], zc[1, h])),
            inner((gg[h], dg[h]), (gc[h], dc[h])),
            inner((w_0, y_0)) * inverse * inverse,
        ])
    for h in range(2):
        face_relay(2, h)
        sums_mid(1, h)

    for h in range(2):
        f_g, f_c = face_end(2, h)
        inverse = 1.0 / scale_of(h)
        imz_g[h] = (imz_g[h] + f_g) * inverse
        imz_c[h] = (imz_c[h] + f_c) * inverse
        face_relay(3, h)
    for h in range(2):
        b_g, b_c = face_end(3, h)
        sums = sums_end(1, h)
        kind = kinds_ref[1:2, cols(h)]
        gamma = jnp.where(kind == 0, sums[0:1] / sums[5:6], 0.0)
        curvature = sums[1:2] - gamma * (sums[2:3] + sums[0:1]) + gamma * gamma * sums[5:6]
        descent = sums[3:4] - gamma * sums[4:5]
        step = jnp.where(kind == 1, 1.0, descent / curvature)
        outg_ref[:, cols(h)] = outg_ref[:, cols(h)] - step * (zg[1, h] - gamma * dg[h])
        outc_ref[:, cols(h)] = outc_ref[:, cols(h)] - step * (zc[1, h] - gamma * dc[h])
        outgg_ref[:, cols(h)] = gg[h] - step * (b_g - gamma * imz_g[h])
        outgc_ref[:, cols(h)] = gc[h] - step * (b_c - gamma * imz_c[h])

    for copy in pending:
        copy.wait_send()
    for there, copy in late:
        @pl.when(there)
        def _(copy=copy):
            copy.wait_send()


def solution(mesh):
    n_bulk, n_group = mesh.shape["bulk"], mesh.shape["contact"]
    split_rows = P(("bulk", "contact"), None)
    ids = P(("bulk", "contact"))
    placed = (split_rows,) * 6 + (ids, ids, P(), P(None, ("bulk", "contact"), None), P())

    def per_device(k_inv, ms, mm, force, lam_g, lam_c, master_map, on_surface, kinds, active, expand_len):
        face, columns = lam_g.shape
        mortar = lam_c.shape[0]
        order = k_inv.shape[1]
        rows = 2 * face + mortar
        half = columns // 2
        slots = n_group - 1
        vmem = pltpu.VMEM
        dma = pltpu.SemaphoreType.DMA
        in_vmem = pl.BlockSpec(memory_space=vmem)
        in_smem = pl.BlockSpec(memory_space=pltpu.SMEM)
        anywhere = pl.BlockSpec(memory_space=pl.ANY)
        dual = lambda *lead: vmem(lead + (2, face, half), F32)
        return tuple(pl.pallas_call(
            functools.partial(kernel, n_bulk, n_group),
            out_shape=[jax.ShapeDtypeStruct((face, columns), F32)] * 4,
            in_specs=[in_smem, in_smem, anywhere, in_vmem, in_vmem, anywhere] + [in_vmem] * 5,
            out_specs=[in_vmem] * 4,
            scratch_shapes=[
                vmem((rows, order), F32), vmem((rows, order), BF16), vmem((rows, order), BF16),
                vmem((order, columns), F32), vmem((order, columns), BF16), vmem((order, columns), BF16),
                vmem((2, rows, half), F32),
                vmem((mortar, 2 * mortar), BF16), vmem((mortar, 2 * mortar), BF16),
                vmem((2 * mortar, mortar), BF16), vmem((2 * mortar, mortar), BF16),
                vmem((2, 2, rows, half), F32), dual(), vmem((4, 2, rows, half), F32),
                dual(3), dual(4), dual(2), dual(2), dual(4),
                vmem((4, 2, slots, mortar, half), F32), vmem((4, 2, slots, mortar, half), F32),
                dual(), dual(), dual(), dual(), dual(), dual(),
                vmem((8, half), F32), vmem((slots, 8, half), F32),
                vmem((2, 2, n_group, 8, half), F32), vmem((2, 2, n_bulk, 8, half), F32),
                dma((2,)), dma((3, 2)), dma((3, 2)), dma((4, 2)), dma((4, 2)),
                dma((4, 2, slots)), dma((4, 2, slots)), dma((4, 2, slots)), dma((4, 2, slots)),
                dma((slots,)), dma((slots,)),
                dma((2, 2, n_group)), dma((2, 2, n_group)), dma((2, 2, n_bulk)), dma((2, 2, n_bulk)),
            ],
            compiler_params=pltpu.CompilerParams(
                collective_id=0, has_side_effects=True, vmem_limit_bytes=60 * 1024 * 1024
            ),
        )(master_map, on_surface, k_inv, ms, mm, force, lam_g, lam_c, kinds, active, expand_len.reshape(1, -1)))

    return jax.shard_map(
        per_device, mesh=mesh, in_specs=placed, out_specs=(split_rows,) * 4, check_vma=False
    )
```

profile of v0, /device:TPU:0, one launch (start us, length us, event | category | flops | bytes accessed | tf_op | source)
XLA Modules:
  0.0 82.2 jit_solution(6606773700443956725)
XLA Ops:
  1.9 73.6 %shard_map.138 = (f32[256,256]{1,0:T(8,128)}, f32[256,256]{1,0:T(8,128)}, f32[256,256]{1,0:T(8,128)}, f32[256,256]{1,0:T(8,128)}) custom-call(s32[1]{0:T(128)S(6)} %copy.19.master_ref, s32[1]{0:T(128)S(6)} %copy.20.surface_ref, f32[2048,2048]{1,0:T(8,128)} %kinv_ref.1, f32[256,256]{1,0:T(8,128)} %ms_ref.1, f32[256,256]{1,0:T(8,128)} %mm_ref.1, ...), custom_call_target="tpu_custom_call" | custom-call | tf_op jit(solution)/shard_map/pallas_call | solution.py:414
  75.5 1.7 %copy.21 = f32[256,256]{1,0:T(8,128)} copy(f32[256,256]{1,0:T(8,128)} %get-tuple-element.8) | data formatting | bytes 524288
  77.2 1.7 %copy.22 = f32[256,256]{1,0:T(8,128)} copy(f32[256,256]{1,0:T(8,128)} %get-tuple-element.9) | data formatting | bytes 524288
  78.9 1.7 %copy.23 = f32[256,256]{1,0:T(8,128)} copy(f32[256,256]{1,0:T(8,128)} %get-tuple-element.10) | data formatting | bytes 524288
  80.5 1.7 %copy.24 = f32[256,256]{1,0:T(8,128)} copy(f32[256,256]{1,0:T(8,128)} %get-tuple-element.11) | data formatting | bytes 524288
where the time goes:
time: 82.5 us; the launch traced here: 82.2 us
  Pallas kernels  73.6 us (89%)
  local copies, waits for them, and re-layouts  6.68 us (8%)
  between operations  1.93 us (2%)
    pallas_call x1, Pallas kernels, per_device(): pl.pallas_call(functools.partial(kernel, n_bulk, n_group), out_shape=[jax...  73.6 us
    unnamed x4, local copies, waits for them, and re-layouts  6.68 us

commit v1 on v0

--- a/solution.py
+++ b/solution.py
@@ -392,6 +392,25 @@
             copy.wait_send()
 
 
+def finish(a, b, c, d, oa, ob, oc, od, sem):
+    copies = [pltpu.make_async_copy(x, y, sem.at[i]) for i, (x, y) in enumerate(((a, oa), (b, ob), (c, oc), (d, od)))]
+    for copy in copies:
+        copy.start()
+    for copy in copies:
+        copy.wait()
+
+
+def settle(parts):
+    shape = jax.ShapeDtypeStruct(parts[0].shape, F32)
+    return tuple(pl.pallas_call(
+        finish,
+        out_shape=[shape] * 4,
+        in_specs=[pl.BlockSpec(memory_space=pltpu.VMEM)] * 4,
+        out_specs=[pl.BlockSpec(memory_space=pl.ANY)] * 4,
+        scratch_shapes=[pltpu.SemaphoreType.DMA((4,))],
+    )(*[pltpu.with_memory_space_constraint(x, pltpu.VMEM) for x in parts]))
+
+
 def solution(mesh):
     n_bulk, n_group = mesh.shape["bulk"], mesh.shape["contact"]
     split_rows = P(("bulk", "contact"), None)
@@ -411,9 +430,9 @@
         in_smem = pl.BlockSpec(memory_space=pltpu.SMEM)
         anywhere = pl.BlockSpec(memory_space=pl.ANY)
         dual = lambda *lead: vmem(lead + (2, face, half), F32)
-        return tuple(pl.pallas_call(
+        return settle(pl.pallas_call(
             functools.partial(kernel, n_bulk, n_group),
-            out_shape=[jax.ShapeDtypeStruct((face, columns), F32)] * 4,
+            out_shape=[pltpu.VMEM((face, columns), F32)] * 4,
             in_specs=[in_smem, in_smem, anywhere, in_vmem, in_vmem, anywhere] + [in_vmem] * 5,
             out_specs=[in_vmem] * 4,
             scratch_shapes=[

time: 82.5 us -> 75.7 us (0.918)
  local copies, waits for them, and re-layouts: 6.68 us -> 0 us
    unnamed x4 -> x0, local copies, waits for them, and re-layouts: 6.68 us -> none
    pallas_call x1 -> x2, Pallas kernels: 73.6 us -> 73.6 us  [the longest x1 72.6 us: per_device(): pl.pallas_call(functools.partial(kernel, n_bulk, n_group), out_shape=[plt...]
where the time goes in v1:
time: 75.7 us; the launch traced here: 75.5 us
  Pallas kernels  73.6 us (97%)
  between operations  1.93 us (3%)
    pallas_call x1, Pallas kernels, per_device(): pl.pallas_call(functools.partial(kernel, n_bulk, n_group), out_shape=[plt...  72.6 us

profile of v1, /device:TPU:0, one launch (start us, length us, event | category | flops | bytes accessed | tf_op | source)
XLA Modules:
  0.0 75.5 jit_solution(11905131900903345414)
XLA Ops:
  1.9 72.6 %shard_map.138 = (f32[256,256]{1,0:T(8,128)S(1)}, f32[256,256]{1,0:T(8,128)S(1)}, f32[256,256]{1,0:T(8,128)S(1)}, f32[256,256]{1,0:T(8,128)S(1)}) custom-call(s32[1]{0:T(128)S(6)} %copy.15.master_ref, s32[1]{0:T(128)S(6)} %copy.16.surface_ref, f32[2048,2048]{1,0:T(8,128)} %kinv_ref.1, f32[256,256]{1,0:T(8,128)} %ms_ref.1, f32[256,256]{1,0:T(8,128)} %mm_ref.1, ...), custom_call_target="tpu_custom_call" | custom-call | tf_op jit(solution)/shard_map/pallas_call | solution.py:433
  74.5 1.0 %shard_map.139 = (f32[256,256]{1,0:T(8,128)}, f32[256,256]{1,0:T(8,128)}, f32[256,256]{1,0:T(8,128)}, f32[256,256]{1,0:T(8,128)}) custom-call(f32[256,256]{1,0:T(8,128)S(1)} %get-tuple-element.8.a, f32[256,256]{1,0:T(8,128)S(1)} %get-tuple-element.9.b, f32[256,256]{1,0:T(8,128)S(1)} %get-tuple-element.10.c, f32[256,256]{1,0:T(8,128)S(1)} %get-tuple-element.11.d), custom_call_target="tpu_custom_call" | custom-call | tf_op jit(solution)/shard_map/pallas_call | solution.py:405

commit v2 on v1

v2 whole, which is shorter than its diff:
```python
import functools

import jax
import jax.numpy as jnp
from jax import lax
from jax.experimental import pallas as pl
from jax.experimental.pallas import tpu as pltpu
from jax.sharding import PartitionSpec as P

MESH = pl.DeviceIdType.MESH
F32 = jnp.float32
BF16 = jnp.bfloat16


def split(x):
    high = x.astype(BF16)
    return high, (x - high.astype(F32)).astype(BF16)


def bdot(a, b):
    return jnp.dot(a, b, preferred_element_type=F32)


def dot3(a_high, a_low, x):
    width = x.shape[1]
    high, low = split(x)
    both = bdot(a_high, jnp.concatenate([high, low], axis=1))
    return both[:, :width] + (both[:, width:] + bdot(a_low, high))


def kernel(
    n_bulk, n_group,
    master_hbm, surface_hbm, kinv_hbm, ms_hbm, mm_hbm, force_hbm, lamg_hbm, lamc_hbm, kinds_hbm, active_hbm, expand_hbm,
    outg_ref, outc_ref, outgg_ref, outgc_ref,
    master_ref, surface_ref, ms_ref, mm_ref, lamg_ref, lamc_ref, kinds_ref, active_ref, expand_ref,
    k_raw, k_hi, k_lo, f_raw, f_hi, f_lo, base, gap_hi, gap_lo, adj_hi, adj_lo,
    w_ref, wfix, y_ref, gp, gl, zg, zc, tsrc, tpart, tout, tin, cpart, cout, cin,
    dg, dc, gg, gc, imz_g, imz_c, own_gap, meta_src, meta, r1, r2,
    load_sem, k_sem, gp_send, gp_recv, gl_send, gl_recv, tp_send, tp_recv, tx_send, tx_recv,
    cp_send, cp_recv, cx_send, cx_recv, m_send, m_recv, r1_send, r1_recv, r2_send, r2_recv,
):
    face, columns = lamg_ref.shape
    mortar = lamc_ref.shape[0]
    rows = 2 * face + mortar
    half = columns // 2
    b = lax.axis_index("bulk")
    c = lax.axis_index("contact")
    pairs = n_group // 2
    q = lax.div(c, 2)
    r = lax.rem(c, 2)
    partner = 2 * q + 1 - r
    pending = []

    barrier = pltpu.get_barrier_semaphore()
    for k in range(1, n_group):
        pl.semaphore_signal(barrier, inc=1, device_id={"bulk": b, "contact": lax.rem(c + k, n_group)}, device_id_type=MESH)
    for k in range(1, n_bulk):
        pl.semaphore_signal(barrier, inc=1, device_id={"bulk": lax.rem(b + k, n_bulk), "contact": c}, device_id_type=MESH)

    def load(i, src, dst):
        copy = pltpu.make_async_copy(src, dst, load_sem.at[i])
        copy.start()
        return copy

    def k_load(i):
        at = pl.ds(pl.multiple_of(i * face, face), face)
        return pltpu.make_async_copy(kinv_hbm.at[at], k_raw.at[at], k_sem.at[i])

    load_mm = load(0, mm_hbm, mm_ref)
    load_lamc = load(1, lamc_hbm, lamc_ref)
    load_master = load(2, master_hbm, master_ref)
    load_surface = load(3, surface_hbm, surface_ref)
    load_lamg = load(4, lamg_hbm, lamg_ref)
    load_ms = load(5, ms_hbm, ms_ref)
    load_f = load(6, force_hbm, f_raw)
    for i in range(3):
        k_load(i).start()
    load_kinds = load(7, kinds_hbm, kinds_ref)
    load_expand = load(8, expand_hbm, expand_ref)
    load_active = load(9, active_hbm, active_ref)

    others = range(1, pairs)

    def other(k):
        return 2 * lax.rem(q + k, pairs) + r

    def remote(src, dst, send, recv, where):
        return pltpu.make_async_remote_copy(
            src_ref=src, dst_ref=dst, send_sem=send, recv_sem=recv, device_id=where, device_id_type=MESH
        )

    def begin(copy):
        copy.start()
        pending.append(copy)

    def near(where):
        return {"bulk": b, "contact": where}

    right = {"bulk": lax.rem(b + 1, n_bulk), "contact": c}
    left = {"bulk": lax.rem(b + n_bulk - 1, n_bulk), "contact": c}
    has_right = b < n_bulk - 1
    has_left = b > 0
    late = []

    def push_glue(src, p, h):
        copy = remote(src, gp.at[p, h], gp_send.at[p, h], gp_recv.at[p, h], right)

        @pl.when(has_right)
        def _():
            copy.start()

        late.append((has_right, copy))

    def push_glue_end(p, h):
        @pl.when(has_left)
        def _():
            remote(gp.at[p, h], gp.at[p, h], gp_send.at[p, h], gp_recv.at[p, h], left).wait_recv()

    def pull_glue(p, h):
        copy = remote(y_ref.at[p, h, pl.ds(0, face)], gl.at[p, h], gl_send.at[p, h], gl_recv.at[p, h], left)

        @pl.when(has_left)
        def _():
            copy.start()

        late.append((has_left, copy))

    def pull_glue_end(p, h):
        @pl.when(has_right)
        def _():
            remote(gl.at[p, h], gl.at[p, h], gl_send.at[p, h], gl_recv.at[p, h], right).wait_recv()

    def cols(h):
        return slice(h * half, (h + 1) * half)

    def pick(row, ident, value):
        return jnp.where(row == ident.astype(F32), value, 0.0)

    def adjoint(parts, first):
        high, low = parts
        cut = pl.ds(first, mortar)
        both = bdot(adj_hi[cut, :], jnp.concatenate([high, low], axis=1))
        return both[:, :half] + (both[:, half:] + bdot(adj_lo[cut, :], high))

    def mortar_swap(p, h):
        begin(remote(tsrc.at[p, h], tpart.at[p, h], tp_send.at[p, h], tp_recv.at[p, h], near(partner)))

    def mortar_cross(p, h):
        remote(tpart.at[p, h], tpart.at[p, h], tp_send.at[p, h], tp_recv.at[p, h], near(partner)).wait_recv()
        for k in others:
            to = other(k)
            tout[p, h, k - 1] = pick(own_row, to, tsrc[p, h]) + pick(meta[0, 0:1, :], to, tpart[p, h])
            begin(remote(tout.at[p, h, k - 1], tin.at[p, h, k - 1], tx_send.at[p, h, k - 1], tx_recv.at[p, h, k - 1], near(to)))

    def mortar_end(p, h):
        total = pick(meta[0, 0:1, :], c, tpart[p, h])
        for k in others:
            remote(tin.at[p, h, k - 1], tin.at[p, h, k - 1], tx_send.at[p, h, k - 1], tx_recv.at[p, h, k - 1],
                   near(other(k))).wait_recv()
            total = total + tin[p, h, k - 1]
        return total

    def face_swap(p, h):
        begin(remote(y_ref.at[p, h, pl.ds(2 * face, mortar)], cpart.at[p, h], cp_send.at[p, h], cp_recv.at[p, h], near(partner)))

    def face_cross(p, h):
        remote(cpart.at[p, h], cpart.at[p, h], cp_send.at[p, h], cp_recv.at[p, h], near(partner)).wait_recv()
        for k in others:
            row = meta[pairs - k, 0:1, :]
            cout[p, h, k - 1] = pick(row, c, y_ref[p, h, 2 * face :, :]) + pick(row, partner, cpart[p, h])
            begin(remote(cout.at[p, h, k - 1], cin.at[p, h, k - 1], cx_send.at[p, h, k - 1], cx_recv.at[p, h, k - 1],
                         near(other(k))))
        own_gap[p, h] = dot3(gap_hi[:, :mortar], gap_lo[:, :mortar], y_ref[p, h, 2 * face :, :])

    def face_end(p, h):
        chosen = pick(own_row, partner, cpart[p, h])
        for k in others:
            remote(cin.at[p, h, k - 1], cin.at[p, h, k - 1], cx_send.at[p, h, k - 1], cx_recv.at[p, h, k - 1],
                   near(other(k))).wait_recv()
            chosen = chosen + cin[p, h, k - 1]
        gap = own_gap[p, h] + dot3(gap_hi[:, mortar:], gap_lo[:, mortar:], chosen)
        pull_glue_end(p, h)
        return (y_ref[p, h, face : 2 * face, :] - gl[p, h]) * mask, gap

    def apply(w_value, p, h, first, plus):
        high, low = split(w_value)
        both = jnp.concatenate([high, low], axis=1)
        cut = pl.ds(first, w_value.shape[0])
        for i in (2, 0, 1):
            at = pl.ds(i * face, face)
            out = bdot(k_hi[at, cut], both)
            out = out[:, :half] + (out[:, half:] + bdot(k_lo[at, cut], high))
            if plus:
                out = out + base[h, at, :]
            y_ref[p, h, at, :] = out
            if i == 2:
                face_swap(p, h)
            if i == 0:
                pull_glue(p, h)

    def sums_start(n, h, values):
        padded = values + [jnp.zeros_like(values[0])] * (8 - len(values))
        r1[n, h, c] = jnp.concatenate(padded, axis=0)
        for k in range(1, n_group):
            begin(remote(r1.at[n, h, c], r1.at[n, h, c], r1_send.at[n, h, k], r1_recv.at[n, h, k],
                         near(lax.rem(c + k, n_group))))

    def sums_mid(n, h):
        for k in range(1, n_group):
            there = lax.rem(c - k + n_group, n_group)
            remote(r1.at[n, h, there], r1.at[n, h, there], r1_send.at[n, h, k], r1_recv.at[n, h, k], near(there)).wait_recv()
        r2[n, h, b] = jnp.sum(r1[n, h], axis=0)
        for k in range(1, n_bulk):
            begin(remote(r2.at[n, h, b], r2.at[n, h, b], r2_send.at[n, h, k], r2_recv.at[n, h, k],
                         {"bulk": lax.rem(b + k, n_bulk), "contact": c}))

    def sums_end(n, h):
        for k in range(1, n_bulk):
            there = lax.rem(b - k + n_bulk, n_bulk)
            remote(r2.at[n, h, there], r2.at[n, h, there], r2_send.at[n, h, k], r2_recv.at[n, h, k],
                   {"bulk": there, "contact": c}).wait_recv()
        return jnp.sum(r2[n, h], axis=0)

    def inner(*terms):
        return sum(jnp.sum(x * y, axis=0, keepdims=True) for x, y in terms)

    load_surface.wait()
    load_mm.wait()
    surface = surface_ref[0].astype(F32)
    mask = jnp.where(has_right, 1.0, 0.0).astype(F32)
    master = mm_ref[...] * surface
    high, low = split(master.T)
    adj_hi[mortar:, :] = high
    adj_lo[mortar:, :] = low
    load_lamc.wait()
    for h in range(2):
        tsrc[0, h] = adjoint(split(lamc_ref[:, cols(h)]), mortar)
    load_master.wait()
    own_master = jnp.full((8, half), master_ref[0].astype(F32), F32)
    own_row = own_master[0:1, :]
    meta_src[...] = own_master
    load_lamg.wait()

    pl.semaphore_wait(barrier, n_group - 1 + n_bulk - 1)
    begin(remote(meta_src, meta.at[0], m_send.at[0], m_recv.at[0], near(partner)))
    for h in range(2):
        mortar_swap(0, h)
    for k in others:
        begin(remote(meta_src, meta.at[k], m_send.at[k], m_recv.at[k], near(other(k))))
    for h in range(2):
        push_glue(lamg_ref.at[:, pl.ds(h * half, half)], 0, h)

    @pl.when(b == 0)
    def _():
        gp[...] = jnp.zeros_like(gp)

    @pl.when(b == n_bulk - 1)
    def _():
        gl[...] = jnp.zeros_like(gl)

    load_ms.wait()
    slave = ms_ref[...] * surface
    high, low = split(slave.T)
    adj_hi[:mortar, :] = high
    adj_lo[:mortar, :] = low
    remote(meta.at[0], meta.at[0], m_send.at[0], m_recv.at[0], near(partner)).wait_recv()
    for h in range(2):
        mortar_cross(0, h)
    for h in range(2):
        w_ref[0, h, 2 * face :, :] = adjoint(split(lamc_ref[:, cols(h)]), 0)
    for i, part in enumerate((slave, -master)):
        high, low = split(part)
        gap_hi[:, i * mortar : (i + 1) * mortar] = high
        gap_lo[:, i * mortar : (i + 1) * mortar] = low

    load_f.wait()
    high, low = split(-f_raw[...])
    f_hi[...] = high
    f_lo[...] = low

    @pl.loop(0, 3)
    def _(i):
        at = pl.ds(pl.multiple_of(i * face, face), face)
        k_load(i).wait()
        high, low = split(k_raw[at, :])
        k_hi[at, :] = high
        k_lo[at, :] = low
        out = bdot(k_hi[at, :], f_hi[...])
        out = out + (bdot(k_hi[at, :], f_lo[...]) + bdot(k_lo[at, :], f_hi[...]))
        for h in range(2):
            base[h, at, :] = out[:, h * half : (h + 1) * half]

    for k in others:
        remote(meta.at[k], meta.at[k], m_send.at[k], m_recv.at[k], near(partner)).wait_recv()
    load_kinds.wait()
    load_expand.wait()
    load_active.wait()

    for h in range(2):
        total = mortar_end(0, h)
        push_glue_end(0, h)
        own = w_ref[0, h, 2 * face :, :]
        w = jnp.concatenate([-gp[0, h], lamg_ref[:, cols(h)] * mask, own - total], axis=0)
        apply(w, 0, h, 0, True)
        face_cross(0, h)

    for h in range(2):
        grad_g, grad_c = face_end(0, h)
        kind = kinds_ref[0:1, cols(h)]
        length = expand_ref[0:1, cols(h)]
        expand = kind == 1
        chop = kind == 2
        held = active_ref[0, :, cols(h)].astype(F32)
        dir_c = jnp.where(chop, jnp.minimum(grad_c, 0.0) * held, grad_c * (1.0 - held)) * surface
        scale = jnp.where(expand, length, 1.0)
        z_c = scale * dir_c
        fix = jnp.where(expand, surface * jnp.maximum(z_c - lamc_ref[:, cols(h)], 0.0), 0.0)
        net = z_c - fix
        parts = split(net)
        tsrc[1, h] = adjoint(parts, mortar)
        mortar_swap(1, h)
        dir_g = jnp.where(chop, 0.0, grad_g)
        zg[0, h] = scale * dir_g
        push_glue(zg.at[0, h], 1, h)
        gg[h] = grad_g
        gc[h] = grad_c
        dg[h] = dir_g
        dc[h] = dir_c
        zc[0, h] = net
        w_ref[0, h, 2 * face :, :] = adjoint(parts, 0)
        parts = split(fix)
        tsrc[2, h] = adjoint(parts, mortar)
        mortar_swap(2, h)
        wfix[h] = adjoint(parts, 0)
        mortar_cross(1, h)

    for h in range(2):
        total = mortar_end(1, h)
        if h == 1:
            sums_mid(0, 0)
        push_glue_end(1, h)
        own = w_ref[0, h, 2 * face :, :]
        w = jnp.concatenate([-gp[1, h], zg[0, h], own - total], axis=0)
        w_ref[0, h] = w
        apply(w, 1, h, 0, False)
        sums_start(0, h, [
            inner((gg[h], dg[h]), (gc[h], dc[h])),
            inner((w, y_ref[1, h])),
        ])
        face_cross(1, h)

    for h in range(2):
        b_g, b_c = face_end(1, h)
        if h == 0:
            sums_mid(0, 1)
        imz_g[h] = b_g
        imz_c[h] = b_c
        sums = sums_end(0, h)
        step = jnp.where(kinds_ref[0:1, cols(h)] == 1, 1.0, sums[0:1] / sums[1:2])
        grad_c = gc[h] - step * b_c
        lam_c = lamc_ref[:, cols(h)] - step * zc[0, h]
        kind = kinds_ref[1:2, cols(h)]
        expand = kind == 1
        chop = kind == 2
        held = active_ref[1, :, cols(h)].astype(F32)
        scale = jnp.where(expand, expand_ref[0:1, cols(h)], 1.0)
        v_c = jnp.where(chop, jnp.minimum(grad_c, 0.0) * held, scale * (grad_c * (1.0 - held))) * surface
        net = v_c - jnp.where(expand, surface * jnp.maximum(v_c - lam_c, 0.0), 0.0)
        parts = split(net)
        tsrc[3, h] = adjoint(parts, mortar)
        mortar_swap(3, h)
        grad_g = gg[h] - step * b_g
        zg[1, h] = jnp.where(chop, 0.0, scale * grad_g)
        push_glue(zg.at[1, h], 2, h)
        zc[1, h] = net
        gg[h] = grad_g
        gc[h] = grad_c
        outg_ref[:, cols(h)] = lamg_ref[:, cols(h)] * mask - step * zg[0, h]
        outc_ref[:, cols(h)] = lam_c
        w_ref[1, h, 2 * face :, :] = adjoint(parts, 0)
        mortar_cross(3, h)
        mortar_cross(2, h)

    def scale_of(h):
        return jnp.where(kinds_ref[0:1, cols(h)] == 1, expand_ref[0:1, cols(h)], 1.0)

    for h in range(2):
        total = mortar_end(3, h)
        push_glue_end(2, h)
        own = w_ref[1, h, 2 * face :, :]
        w = jnp.concatenate([-gp[2, h], zg[1, h], own - total], axis=0)
        w_ref[1, h] = w
        apply(w, 3, h, 0, False)
        face_cross(3, h)
        w_f = wfix[h] - mortar_end(2, h)
        if h == 1:
            sums_mid(1, 0)
        apply(w_f, 2, h, 2 * face, False)
        w = w_ref[1, h]
        w_0 = jnp.concatenate([w_ref[0, h, : 2 * face, :], w_ref[0, h, 2 * face :, :] + w_f], axis=0)
        y_0 = y_ref[1, h] + y_ref[2, h]
        inverse = 1.0 / scale_of(h)
        y_v = y_ref[3, h]
        sums_start(1, h, [
            inner((w, y_0)) * inverse,
            inner((w, y_v)),
            inner((w_0, y_v)) * inverse,
            inner((gg[h], zg[1, h]), (gc[h], zc[1, h])),
            inner((gg[h], dg[h]), (gc[h], dc[h])),
            inner((w_0, y_0)) * inverse * inverse,
        ])
        face_cross(2, h)

    for h in range(2):
        b_g, b_c = face_end(3, h)
        f_g, f_c = face_end(2, h)
        if h == 0:
            sums_mid(1, 1)
        sums = sums_end(1, h)
        inverse = 1.0 / scale_of(h)
        kind = kinds_ref[1:2, cols(h)]
        gamma = jnp.where(kind == 0, sums[0:1] / sums[5:6], 0.0)
        curvature = sums[1:2] - gamma * (sums[2:3] + sums[0:1]) + gamma * gamma * sums[5:6]
        descent = sums[3:4] - gamma * sums[4:5]
        step = jnp.where(kind == 1, 1.0, descent / curvature)
        outg_ref[:, cols(h)] = outg_ref[:, cols(h)] - step * (zg[1, h] - gamma * dg[h])
        outc_ref[:, cols(h)] = outc_ref[:, cols(h)] - step * (zc[1, h] - gamma * dc[h])
        outgg_ref[:, cols(h)] = gg[h] - step * (b_g - gamma * ((imz_g[h] + f_g) * inverse))
        outgc_ref[:, cols(h)] = gc[h] - step * (b_c - gamma * ((imz_c[h] + f_c) * inverse))

    for copy in pending:
        copy.wait_send()
    for there, copy in late:
        @pl.when(there)
        def _(copy=copy):
            copy.wait_send()


def finish(a, b, c, d, oa, ob, oc, od, sem):
    copies = [pltpu.make_async_copy(x, y, sem.at[i]) for i, (x, y) in enumerate(((a, oa), (b, ob), (c, oc), (d, od)))]
    for copy in copies:
        copy.start()
    for copy in copies:
        copy.wait()


def settle(parts):
    shape = jax.ShapeDtypeStruct(parts[0].shape, F32)
    return tuple(pl.pallas_call(
        finish,
        out_shape=[shape] * 4,
        in_specs=[pl.BlockSpec(memory_space=pltpu.VMEM)] * 4,
        out_specs=[pl.BlockSpec(memory_space=pl.ANY)] * 4,
        scratch_shapes=[pltpu.SemaphoreType.DMA((4,))],
    )(*[pltpu.with_memory_space_constraint(x, pltpu.VMEM) for x in parts]))


def solution(mesh):
    n_bulk, n_group = mesh.shape["bulk"], mesh.shape["contact"]
    split_rows = P(("bulk", "contact"), None)
    ids = P(("bulk", "contact"))
    placed = (split_rows,) * 6 + (ids, ids, P(), P(None, ("bulk", "contact"), None), P())

    def per_device(k_inv, ms, mm, force, lam_g, lam_c, master_map, on_surface, kinds, active, expand_len):
        face, columns = lam_g.shape
        mortar = lam_c.shape[0]
        order = k_inv.shape[1]
        rows = 2 * face + mortar
        half = columns // 2
        cross = n_group // 2 - 1
        vmem = pltpu.VMEM
        dma = pltpu.SemaphoreType.DMA
        in_vmem = pl.BlockSpec(memory_space=vmem)
        anywhere = pl.BlockSpec(memory_space=pl.ANY)
        dual = lambda *lead: vmem(lead + (2, face, half), F32)
        lanes = lambda lead, *rest: vmem((lead, 2) + rest + (mortar, half), F32)
        pair_sems = lambda *dims: [dma(dims), dma(dims)]
        expand_len = expand_len.reshape(1, -1)
        return settle(pl.pallas_call(
            functools.partial(kernel, n_bulk, n_group),
            out_shape=[vmem((face, columns), F32)] * 4,
            in_specs=[anywhere] * 11,
            out_specs=[in_vmem] * 4,
            scratch_shapes=[
                pltpu.SMEM(master_map.shape, jnp.int32), pltpu.SMEM(on_surface.shape, jnp.int32),
                vmem(ms.shape, F32), vmem(mm.shape, F32), vmem(lam_g.shape, F32), vmem(lam_c.shape, F32),
                vmem(kinds.shape, jnp.int32), vmem(active.shape, jnp.int32), vmem(expand_len.shape, F32),
                vmem((rows, order), F32), vmem((rows, order), BF16), vmem((rows, order), BF16),
                vmem((order, columns), F32), vmem((order, columns), BF16), vmem((order, columns), BF16),
                vmem((2, rows, half), F32),
                vmem((mortar, 2 * mortar), BF16), vmem((mortar, 2 * mortar), BF16),
                vmem((2 * mortar, mortar), BF16), vmem((2 * mortar, mortar), BF16),
                vmem((2, 2, rows, half), F32), dual(), vmem((4, 2, rows, half), F32),
                dual(3), dual(4), dual(2), dual(2),
                lanes(4), lanes(4), lanes(4, cross), lanes(4, cross), lanes(4), lanes(4, cross), lanes(4, cross),
                dual(), dual(), dual(), dual(), dual(), dual(), dual(4),
                vmem((8, half), F32), vmem((n_group // 2, 8, half), F32),
                vmem((2, 2, n_group, 8, half), F32), vmem((2, 2, n_bulk, 8, half), F32),
                dma((10,)), dma((3,)), *pair_sems(3, 2), *pair_sems(4, 2),
                *pair_sems(4, 2), *pair_sems(4, 2, cross), *pair_sems(4, 2), *pair_sems(4, 2, cross),
                *pair_sems(n_group // 2), *pair_sems(2, 2, n_group), *pair_sems(2, 2, n_bulk),
            ],
            compiler_params=pltpu.CompilerParams(
                collective_id=0, has_side_effects=True, vmem_limit_bytes=60 * 1024 * 1024
            ),
        )(master_map, on_surface, k_inv, ms, mm, force, lam_g, lam_c, kinds, active, expand_len))

    return jax.shard_map(
        per_device, mesh=mesh, in_specs=placed, out_specs=(split_rows,) * 4, check_vma=False
    )
```

time: 75.7 us -> 65.4 us (0.86)
  Pallas kernels: 73.6 us -> 63.2 us
    pallas_call x1, Pallas kernels: 72.6 us -> 62.2 us  [per_device(): pl.pallas_call(functools.partial(kernel, n_bulk, n_group), out_shape=[vme...]
where the time goes in v2:
time: 65.4 us; the launch traced here: 65.3 us
  Pallas kernels  63.2 us (97%)
  between operations  2.09 us (3%)
    pallas_call x1, Pallas kernels, per_device(): pl.pallas_call(functools.partial(kernel, n_bulk, n_group), out_shape=[vme...  62.2 us

profile of v2, /device:TPU:0, one launch (start us, length us, event | category | flops | bytes accessed | tf_op | source)
XLA Modules:
  0.0 65.3 jit_solution(9472713922718746347)
XLA Ops:
  1.9 62.2 %shard_map.138 = (f32[256,256]{1,0:T(8,128)S(1)}, f32[256,256]{1,0:T(8,128)S(1)}, f32[256,256]{1,0:T(8,128)S(1)}, f32[256,256]{1,0:T(8,128)S(1)}) custom-call(s32[1]{0:T(128)S(6)} %copy.15.master_hbm, s32[1]{0:T(128)S(6)} %copy.16.surface_hbm, f32[2048,2048]{1,0:T(8,128)} %kinv_hbm.1, f32[256,256]{1,0:T(8,128)} %ms_hbm.1, f32[256,256]{1,0:T(8,128)} %mm_hbm.1, ...), custom_call_target="tpu_custom_call" | custom-call | tf_op jit(solution)/shard_map/pallas_call | solution.py:479
  64.1 1.0 %shard_map.139 = (f32[256,256]{1,0:T(8,128)}, f32[256,256]{1,0:T(8,128)}, f32[256,256]{1,0:T(8,128)}, f32[256,256]{1,0:T(8,128)}) custom-call(f32[256,256]{1,0:T(8,128)S(1)} %get-tuple-element.8.a, f32[256,256]{1,0:T(8,128)S(1)} %get-tuple-element.9.b, f32[256,256]{1,0:T(8,128)S(1)} %get-tuple-element.10.c, f32[256,256]{1,0:T(8,128)S(1)} %get-tuple-element.11.d), custom_call_target="tpu_custom_call" | custom-call | tf_op jit(solution)/shard_map/pallas_call | solution.py:449

commit v3 on v2

--- a/solution.py
+++ b/solution.py
@@ -72,12 +72,6 @@
     load_surface = load(3, surface_hbm, surface_ref)
     load_lamg = load(4, lamg_hbm, lamg_ref)
     load_ms = load(5, ms_hbm, ms_ref)
-    load_f = load(6, force_hbm, f_raw)
-    for i in range(3):
-        k_load(i).start()
-    load_kinds = load(7, kinds_hbm, kinds_ref)
-    load_expand = load(8, expand_hbm, expand_ref)
-    load_active = load(9, active_hbm, active_ref)
 
     others = range(1, pairs)
 
@@ -182,7 +176,7 @@
         pull_glue_end(p, h)
         return (y_ref[p, h, face : 2 * face, :] - gl[p, h]) * mask, gap
 
-    def apply(w_value, p, h, first, plus):
+    def apply(w_value, p, h, first, plus, send=True, between=None):
         high, low = split(w_value)
         both = jnp.concatenate([high, low], axis=1)
         cut = pl.ds(first, w_value.shape[0])
@@ -193,9 +187,11 @@
             if plus:
                 out = out + base[h, at, :]
             y_ref[p, h, at, :] = out
-            if i == 2:
+            if send and i == 2:
                 face_swap(p, h)
-            if i == 0:
+            if between is not None and i == 2:
+                between()
+            if send and i == 0:
                 pull_glue(p, h)
 
     def sums_start(n, h, values):
@@ -224,8 +220,14 @@
     def inner(*terms):
         return sum(jnp.sum(x * y, axis=0, keepdims=True) for x, y in terms)
 
+    load_mm.wait()
     load_surface.wait()
-    load_mm.wait()
+    load_f = load(6, force_hbm, f_raw)
+    for i in range(3):
+        k_load(i).start()
+    load_kinds = load(7, kinds_hbm, kinds_ref)
+    load_expand = load(8, expand_hbm, expand_ref)
+    load_active = load(9, active_hbm, active_ref)
     surface = surface_ref[0].astype(F32)
     mask = jnp.where(has_right, 1.0, 0.0).astype(F32)
     master = mm_ref[...] * surface
@@ -336,13 +338,11 @@
 
     for h in range(2):
         total = mortar_end(1, h)
-        if h == 1:
-            sums_mid(0, 0)
         push_glue_end(1, h)
         own = w_ref[0, h, 2 * face :, :]
         w = jnp.concatenate([-gp[1, h], zg[0, h], own - total], axis=0)
         w_ref[0, h] = w
-        apply(w, 1, h, 0, False)
+        apply(w, 1, h, 0, False, True, (lambda: sums_mid(0, 0)) if h == 1 else None)
         sums_start(0, h, [
             inner((gg[h], dg[h]), (gc[h], dc[h])),
             inner((w, y_ref[1, h])),
@@ -351,10 +351,10 @@
 
     for h in range(2):
         b_g, b_c = face_end(1, h)
-        if h == 0:
-            sums_mid(0, 1)
-        imz_g[h] = b_g
-        imz_c[h] = b_c
+        if h == 1:
+            mortar_cross(2, 0)
+            imz_g[...] = b_g
+            imz_c[...] = b_c
         sums = sums_end(0, h)
         step = jnp.where(kinds_ref[0:1, cols(h)] == 1, 1.0, sums[0:1] / sums[1:2])
         grad_c = gc[h] - step * b_c
@@ -369,6 +369,8 @@
         parts = split(net)
         tsrc[3, h] = adjoint(parts, mortar)
         mortar_swap(3, h)
+        if h == 0:
+            sums_mid(0, 1)
         grad_g = gg[h] - step * b_g
         zg[1, h] = jnp.where(chop, 0.0, scale * grad_g)
         push_glue(zg.at[1, h], 2, h)
@@ -379,25 +381,13 @@
         outc_ref[:, cols(h)] = lam_c
         w_ref[1, h, 2 * face :, :] = adjoint(parts, 0)
         mortar_cross(3, h)
-        mortar_cross(2, h)
 
     def scale_of(h):
         return jnp.where(kinds_ref[0:1, cols(h)] == 1, expand_ref[0:1, cols(h)], 1.0)
 
-    for h in range(2):
-        total = mortar_end(3, h)
-        push_glue_end(2, h)
-        own = w_ref[1, h, 2 * face :, :]
-        w = jnp.concatenate([-gp[2, h], zg[1, h], own - total], axis=0)
-        w_ref[1, h] = w
-        apply(w, 3, h, 0, False)
-        face_cross(3, h)
-        w_f = wfix[h] - mortar_end(2, h)
-        if h == 1:
-            sums_mid(1, 0)
-        apply(w_f, 2, h, 2 * face, False)
+    def step_sums(h):
         w = w_ref[1, h]
-        w_0 = jnp.concatenate([w_ref[0, h, : 2 * face, :], w_ref[0, h, 2 * face :, :] + w_f], axis=0)
+        w_0 = jnp.concatenate([w_ref[0, h, : 2 * face, :], w_ref[0, h, 2 * face :, :] + wfix[h]], axis=0)
         y_0 = y_ref[1, h] + y_ref[2, h]
         inverse = 1.0 / scale_of(h)
         y_v = y_ref[3, h]
@@ -409,24 +399,59 @@
             inner((gg[h], dg[h]), (gc[h], dc[h])),
             inner((w_0, y_0)) * inverse * inverse,
         ])
-        face_cross(2, h)
-
-    for h in range(2):
-        b_g, b_c = face_end(3, h)
-        f_g, f_c = face_end(2, h)
-        if h == 0:
-            sums_mid(1, 1)
+
+    def step_end(h):
         sums = sums_end(1, h)
-        inverse = 1.0 / scale_of(h)
         kind = kinds_ref[1:2, cols(h)]
         gamma = jnp.where(kind == 0, sums[0:1] / sums[5:6], 0.0)
         curvature = sums[1:2] - gamma * (sums[2:3] + sums[0:1]) + gamma * gamma * sums[5:6]
         descent = sums[3:4] - gamma * sums[4:5]
-        step = jnp.where(kind == 1, 1.0, descent / curvature)
+        return gamma, jnp.where(kind == 1, 1.0, descent / curvature)
+
+    def move(h, gamma, step):
         outg_ref[:, cols(h)] = outg_ref[:, cols(h)] - step * (zg[1, h] - gamma * dg[h])
         outc_ref[:, cols(h)] = outc_ref[:, cols(h)] - step * (zc[1, h] - gamma * dc[h])
-        outgg_ref[:, cols(h)] = gg[h] - step * (b_g - gamma * ((imz_g[h] + f_g) * inverse))
-        outgc_ref[:, cols(h)] = gc[h] - step * (b_c - gamma * ((imz_c[h] + f_c) * inverse))
+
+    for h in range(2):
+        total = mortar_end(3, h)
+        push_glue_end(2, h)
+        own = w_ref[1, h, 2 * face :, :]
+        w = jnp.concatenate([-gp[2, h], zg[1, h], own - total], axis=0)
+        w_ref[1, h] = w
+        apply(w, 3, h, 0, False, h == 1, (lambda: sums_mid(1, 0)) if h == 1 else None)
+        if h == 1:
+            face_cross(3, h)
+        w_f = wfix[h] - mortar_end(2, h)
+        wfix[h] = w_f
+        apply(w_f, 2, h, 2 * face, False, h == 1)
+        step_sums(h)
+        if h == 0:
+            mortar_cross(2, 1)
+
+    gamma_first, step_first = step_end(0)
+    back = gamma_first / scale_of(0)
+    for i in (2, 0, 1):
+        at = pl.ds(i * face, face)
+        y_ref[3, 0, at, :] = y_ref[3, 0, at, :] - back * (y_ref[1, 0, at, :] + y_ref[2, 0, at, :])
+        if i == 2:
+            face_swap(3, 0)
+        if i == 0:
+            pull_glue(3, 0)
+    face_cross(2, 1)
+    face_cross(3, 0)
+    sums_mid(1, 1)
+    move(0, gamma_first, step_first)
+
+    b_g, b_c = face_end(3, 1)
+    f_g, f_c = face_end(2, 1)
+    gamma, step = step_end(1)
+    back = gamma / scale_of(1)
+    outgg_ref[:, cols(1)] = gg[1] - step * (b_g - back * (imz_g[...] + f_g))
+    outgc_ref[:, cols(1)] = gc[1] - step * (b_c - back * (imz_c[...] + f_c))
+    move(1, gamma, step)
+    b_g, b_c = face_end(3, 0)
+    outgg_ref[:, cols(0)] = gg[0] - step_first * b_g
+    outgc_ref[:, cols(0)] = gc[0] - step_first * b_c
 
     for copy in pending:
         copy.wait_send()
@@ -493,7 +518,7 @@
                 vmem((2, 2, rows, half), F32), dual(), vmem((4, 2, rows, half), F32),
                 dual(3), dual(4), dual(2), dual(2),
                 lanes(4), lanes(4), lanes(4, cross), lanes(4, cross), lanes(4), lanes(4, cross), lanes(4, cross),
-                dual(), dual(), dual(), dual(), dual(), dual(), dual(4),
+                dual(), dual(), dual(), dual(), vmem((face, half), F32), vmem((mortar, half), F32), dual(4),
                 vmem((8, half), F32), vmem((n_group // 2, 8, half), F32),
                 vmem((2, 2, n_group, 8, half), F32), vmem((2, 2, n_bulk, 8, half), F32),
                 dma((10,)), dma((3,)), *pair_sems(3, 2), *pair_sems(4, 2),

time: 65.4 us -> 62.6 us (0.957)
  Pallas kernels: 63.2 us -> 60.3 us
    pallas_call x1, Pallas kernels: 62.2 us -> 59.3 us  [per_device(): pl.pallas_call(functools.partial(kernel, n_bulk, n_group), out_shape=[vme...]
where the time goes in v3:
time: 62.6 us; the launch traced here: 62.4 us
  Pallas kernels  60.3 us (96%)
  between operations  2.09 us (3%)
    pallas_call x1, Pallas kernels, per_device(): pl.pallas_call(functools.partial(kernel, n_bulk, n_group), out_shape=[vme...  59.3 us

profile of v3, /device:TPU:0, one launch (start us, length us, event | category | flops | bytes accessed | tf_op | source)
XLA Modules:
  0.0 62.4 jit_solution(11564685902394255518)
XLA Ops:
  1.9 59.3 %shard_map.138 = (f32[256,256]{1,0:T(8,128)S(1)}, f32[256,256]{1,0:T(8,128)S(1)}, f32[256,256]{1,0:T(8,128)S(1)}, f32[256,256]{1,0:T(8,128)S(1)}) custom-call(s32[1]{0:T(128)S(6)} %copy.15.master_hbm, s32[1]{0:T(128)S(6)} %copy.16.surface_hbm, f32[2048,2048]{1,0:T(8,128)} %kinv_hbm.1, f32[256,256]{1,0:T(8,128)} %ms_hbm.1, f32[256,256]{1,0:T(8,128)} %mm_hbm.1, ...), custom_call_target="tpu_custom_call" | custom-call | tf_op jit(solution)/shard_map/pallas_call | solution.py:504
  61.3 1.0 %shard_map.139 = (f32[256,256]{1,0:T(8,128)}, f32[256,256]{1,0:T(8,128)}, f32[256,256]{1,0:T(8,128)}, f32[256,256]{1,0:T(8,128)}) custom-call(f32[256,256]{1,0:T(8,128)S(1)} %get-tuple-element.8.a, f32[256,256]{1,0:T(8,128)S(1)} %get-tuple-element.9.b, f32[256,256]{1,0:T(8,128)S(1)} %get-tuple-element.10.c, f32[256,256]{1,0:T(8,128)S(1)} %get-tuple-element.11.d), custom_call_target="tpu_custom_call" | custom-call | tf_op jit(solution)/shard_map/pallas_call | solution.py:474
